TPU v7x, 128 devices: a whole 4x4x4 slice. The times are simulated.
128 devices in a mesh: fsdp: 32 (over x_hi, y, z), ctx: 4 (over x_lo, core).
Axes of the slice: x: 4 (x_hi: 2, x_lo: 2; x = x_hi * 2 + x_lo), y: 4, z: 4, core: 2. Of those that a mesh axis runs over, the one named last changes fastest.
Arguments:
- token_ids: int32 [32, 512], P('fsdp', 'ctx'), may hold values from 0 to 511
- embedding: bfloat16 [512, 4096], replicated, may hold values from -15 to 15
- norm_gain: float32 [4096], replicated, may hold values from 0.5 to 1.5
- in_proj: bfloat16 [3, 4096, 4096], P(None, None, 'fsdp'), may hold values from -0.09375 to 0.09375
- short_taps: float32 [3, 3, 4096], P(None, None, 'fsdp'), may hold values from -3 to 3
- conv_taps: bfloat16 [256, 128], P('fsdp'), may hold values from -0.6 to 0.6
- out_proj: bfloat16 [4096, 4096], P('fsdp'), may hold values from -0.09375 to 0.09375
Outputs:
- output: bfloat16 [32, 512, 4096], P('fsdp', 'ctx')
All inputs are finite; a program needn't handle non-finite values.
Results may differ from a plain program's by a relative error of at most 0.02.
Values may be sent and summed in bfloat16 or wider, within the bound.
A program may use at most 128 MiB of HBM per device.

v0:
```python
import jax
import jax.numpy as jnp
from jax import lax
from jax.sharding import PartitionSpec as P

GROUP = 16
TAPS = 128
SHORT = 3


def laid_out(blocks, dim):
    lengths = list(blocks.shape[1:])
    lengths[dim] *= blocks.shape[0]
    return jnp.moveaxis(blocks, 0, dim).reshape(lengths)


def from_everyone(x, axis):
    peers = lax.axis_size(axis)
    return lax.all_to_all(jnp.broadcast_to(x[None], (peers, *x.shape)), axis, 0, 0, tiled=True)


def collect(x, axis, dim):
    return laid_out(from_everyone(x, axis), dim)


def from_behind(x, axis, by):
    peers = lax.axis_size(axis)
    pairs = [(i, i + by) for i in range(peers) if 0 <= i + by < peers]
    return lax.ppermute(x, axis, pairs)


def normalize_rows(table_rows, norm_gain):
    values = table_rows.astype(jnp.float32)
    inverse_rms = lax.rsqrt(jnp.mean(values * values, axis=-1, keepdims=True) + 1e-06)
    return (values * inverse_rms * norm_gain).astype(jnp.bfloat16)


def per_device(token_ids, embedding, norm_gain, in_proj, short_taps, conv_taps, out_proj):
    tok_len = token_ids.shape[1]
    panel_width = out_proj.shape[0]
    short_reach = SHORT - 1
    long_reach = TAPS - 1
    all_ids = collect(token_ids, "fsdp", 0)
    windows = all_ids.shape[0]
    normed = normalize_rows(embedding, norm_gain)
    proj_table = jnp.einsum(
        "vd,idc->ivc", normed, in_proj, preferred_element_type=jnp.float32
    ).astype(jnp.bfloat16)
    projected = jnp.take(proj_table, all_ids, axis=1)
    prior_rows = from_behind(projected[:, :, tok_len - short_reach :, :], "ctx", 1)
    extended = jnp.concatenate([prior_rows, projected], axis=2)
    featured = jnp.zeros(projected.shape, jnp.float32)
    for offset in range(SHORT):
        shifted = extended[:, :, short_reach - offset : short_reach - offset + tok_len, :].astype(
            jnp.float32
        )
        featured = featured + short_taps[offset][:, None, None, :] * shifted
    product = (featured[1] * featured[2]).astype(jnp.bfloat16)
    prior_products = from_behind(product[:, tok_len - long_reach :, :], "ctx", 1)
    with_rim = jnp.concatenate([prior_products, product], axis=1)
    lag_grid = jnp.arange(tok_len)[:, None] + long_reach - jnp.arange(tok_len + long_reach)[None, :]
    in_reach = (lag_grid >= 0) & (lag_grid < TAPS)
    toeplitz = jnp.where(
        in_reach[None],
        jnp.take(conv_taps, jnp.clip(lag_grid, 0, TAPS - 1), axis=1),
        jnp.zeros((), jnp.bfloat16),
    )
    groups_dev = conv_taps.shape[0]
    grouped = with_rim.reshape(windows, tok_len + long_reach, groups_dev, GROUP)
    filtered = jnp.einsum("gts,wsgc->wtgc", toeplitz, grouped, preferred_element_type=jnp.float32)
    filtered = filtered.reshape(windows, tok_len, panel_width)
    gated = (featured[0] * filtered).astype(jnp.bfloat16)
    token_major = lax.all_to_all(gated, "fsdp", split_axis=0, concat_axis=2, tiled=True)[0]
    starting = jnp.zeros((tok_len, token_major.shape[1]), jnp.float32)
    running = starting
    weight_piece = lax.all_gather(out_proj, "fsdp", axis=0, tiled=True)
    blocks = weight_piece.shape[0] // panel_width
    col_blocks = jnp.transpose(token_major.reshape(tok_len, blocks, panel_width), (1, 0, 2))
    row_blocks = weight_piece.reshape(blocks, panel_width, weight_piece.shape[1])

    def add_block(partial_sum, block_pair):
        block_out = jnp.dot(
            block_pair[0], block_pair[1], preferred_element_type=jnp.float32
        ).astype(jnp.bfloat16)
        block_out = lax.optimization_barrier(block_out)
        return (partial_sum + block_out.astype(jnp.float32), None)

    running, unused = lax.scan(add_block, running, (col_blocks, row_blocks))
    residual = jnp.take(embedding, token_ids[0], axis=0).astype(jnp.float32)
    return (residual + running).astype(jnp.bfloat16)[None]


def solution(mesh):
    return jax.shard_map(
        per_device,
        mesh=mesh,
        in_specs=(
            P("fsdp", "ctx"),
            P(),
            P(),
            P(None, None, "fsdp"),
            P(None, None, "fsdp"),
            P("fsdp", None),
            P("fsdp", None),
        ),
        out_specs=P("fsdp", "ctx", None),
        check_vma=False,
    )
```

profile of v0, /device:TPU:1, one launch (start us, length us, event | category | flops | bytes accessed | tf_op | source)
XLA Modules:
  0.0 450.6 jit_solution(17973763406091826021)
XLA Ops:
  8.8 11.3 %all-to-all-start = ((s32[32,1,128]{2,1,0:T(1,128)}), s32[32,1,128]{2,1,0:T(1,128)S(1)}, u32[]{:S(2)}, u32[]{:S(2)}) async-start(s32[32,1,128]{2,1,0:T(1,128)} %broadcast_in_dim.62), calls=%async_computation | async-start | bytes 32768 | tf_op jit(solution)/shard_map/all_to_all | solution.py:19
  20.1 3.2 fusion.5
  28.7 28.4 %gather_fusion.1 = bf16[4096,3,128]{2,1,0:T(4,128)(2,1)} fusion(bf16[3,512,128]{2,0,1:T(4,128)(2,1)S(1)} %copy.17, s32[4096]{0:T(1024)S(1)} %fusion.44), kind=kCustom, calls=%fused_computation.1 | custom fusion | bytes 6307840 | tf_op jit(solution)/shard_map/jit(_take)/gather | solution.py:49
  57.1 7.1 %copy.18 = bf16[32,128,3,128]{1,3,0,2:T(8,128)(2,1)} copy(bf16[32,128,3,128]{3,2,1,0:T(4,128)(2,1)} %bitcast.69) | data formatting | bytes 6291456 | tf_op jit(solution)/shard_map/jit(_take)/gather | solution.py:49
  69.1 3.2 copy.19
  72.3 4.2 collective-permute-start
  81.5 6.5 %multiply_add_fusion = f32[3,32,128,128]{2,3,1,0:T(8,128)S(1)} fusion(bf16[3,32,128,128]{2,3,1,0:T(8,128)(2,1)S(1)} %select_bitcast_fusion, bf16[3,32,2,128]{2,3,1,0:T(8,128)(2,1)} %copy.20, f32[3,128]{1,0:T(4,128)S(1)} %get-tuple-element.60, f32[3,128]{1,0:T(4,128)S(1)} %get-tuple-element.61, f32[3,128]{1,0:T(4,128)S(1)} %get-tuple-element.59), kind=kLoop, calls=%fused_computation.17 | loop fusion | flops 22020096 | bytes 9490944 | tf_op jit(solution)/shard_map/add | solution.py:57
  93.2 4.9 %collective-permute-start.1 = (bf16[32,127,128]{2,0,1:T(8,128)(2,1)}, bf16[32,127,128]{2,0,1:T(8,128)(2,1)}, u32[]{:S(2)}, u32[]{:S(2)}) collective-permute-start(bf16[32,127,128]{2,0,1:T(8,128)(2,1)} %copy.21), channel_id=1, source_target_pairs={{0,1},{1,2},{2,3},{4,5},{5,6},{6,7},{8,9},{9,10},{10,11},{12,13},{... | collective-permute-start | bytes 3121160 | tf_op jit(solution)/shard_map/ppermute | solution.py:29
  98.8 66.0 %gather_fusion.2 = bf16[32640,8]{1,0:T(8,128)(2,1)} fusion(bf16[8,128]{0,1:T(8,128)(2,1)S(1)} %copy.23, s32[32768]{0:T(1024)S(1)} %pad_clamp_fusion), kind=kCustom, calls=%fused_computation.2 | custom fusion | bytes 1175040 | tf_op jit(solution)/shard_map/jit(_take)/gather | solution.py:65
  164.7 6.3 %copy.24 = bf16[32640,8]{0,1:T(8,128)(2,1)S(1)} copy(bf16[32640,8]{1,0:T(8,128)(2,1)} %gather_fusion.2) | data formatting | bytes 1044480 | tf_op jit(solution)/shard_map/jit(_take)/gather | solution.py:65
  179.5 6.4 %all-to-all-start.1 = ((bf16[32,128,128]{1,2,0:T(8,128)(2,1)}), bf16[32,128,128]{1,2,0:T(8,128)(2,1)S(1)}, u32[]{:S(2)}, u32[]{:S(2)}) async-start(bf16[32,128,128]{1,2,0:T(8,128)(2,1)} %fusion.16), calls=%async_computation.1 | async-start | bytes 2097152 | tf_op jit(solution)/shard_map/all_to_all | solution.py:73
  186.0 5.9 %gather_fusion = bf16[128,4096]{1,0:T(8,128)(2,1)} fusion(bf16[512,4096]{1,0:T(8,128)(2,1)} %param.10, s32[1024]{0:T(1024)S(1)} %pad_clamp_fusion.1), kind=kCustom, calls=%fused_computation | custom fusion | bytes 2097664 | tf_op jit(solution)/shard_map/jit(_take)/gather | solution.py:89
  191.9 22.0 %all-to-all-done.1 = bf16[32,128,128]{1,2,0:T(8,128)(2,1)S(1)} async-done(((bf16[32,128,128]{1,2,0:T(8,128)(2,1)}), bf16[32,128,128]{1,2,0:T(8,128)(2,1)S(1)}, u32[]{:S(2)}, u32[]{:S(2)}) %all-to-all-start.1) | async-done | bytes 1048608 | tf_op jit(solution)/shard_map/all_to_all | solution.py:73
  213.9 72.4 %all-gather.2.cloned.1.call-done = bf16[4096,4096]{1,0:T(8,128)(2,1)} async-done(((bf16[128,4096]{1,0:T(8,128)(2,1)}), bf16[4096,4096]{1,0:T(8,128)(2,1)}) %all-gather.2.cloned.1.call-update) | async-done | bytes 33554448 | tf_op jit(solution)/shard_map/all_gather | solution.py:76
  286.2 154.2 %while.11 = (s32[]{:T(128)}, f32[128,4096]{1,0:T(8,128)}, bf16[32,128,128]{1,2,0:T(8,128)(2,1)S(1)}, bf16[32,128,4096]{2,1,0:T(8,128)(2,1)}, s32[]{:T(128)}, /*index=5*/s32[]{:T(128)}) while((s32[]{:T(128)}, f32[128,4096]{1,0:T(8,128)}, bf16[32,128,128]{1,2,0:T(8,128)(2,1)S(1)}, bf16[32,128,4096]{2,1,0:T(8,128)(2,1)}, s32[]{:T(128)}, ...), condition=%wide.region_2.3_spmd.clone, body=%wide.region_1.2_spmd.clone.sunk | while | flops 136314880 | bytes 7373903 | solution.py:88
  291.2 3.2 select_add_fusion.2
  300.9 3.2 select_add_fusion.2
  305.8 3.2 select_add_fusion.2
  320.4 3.2 select_add_fusion.2
  339.9 3.2 select_add_fusion.2
  344.8 3.2 select_add_fusion.2
  349.6 3.2 select_add_fusion.2
  364.2 3.2 select_add_fusion.2
  440.5 3.3 fusion.28
  (106 shorter events, 160.0 us)
Async XLA Ops:
  6.5 16.8 %copy-start = (bf16[3,4096,128]{2,1,0:T(8,128)(2,1)S(1)}, bf16[3,4096,128]{2,1,0:T(8,128)(2,1)}, u32[]{:S(2)}) copy-start(bf16[3,4096,128]{2,1,0:T(8,128)(2,1)} %param.12) | copy-start | bytes 9437188
  6.5 16.8 %copy-start.7 = (f32[4096]{0:T(1024)S(1)}, f32[4096]{0:T(1024)}, u32[]{:S(2)}) copy-start(f32[4096]{0:T(1024)} %param.11) | copy-start | bytes 49156
  6.5 279.7 %all-gather.2.cloned.1.call-start = ((), (), s32[]{:S(2)}) async-start(), calls=%async_computation.2 | async-start | bytes 34603008 | tf_op jit(solution)/shard_map/all_gather | solution.py:76
  8.8 19.9 %all-to-all-start = ((s32[32,1,128]{2,1,0:T(1,128)}), s32[32,1,128]{2,1,0:T(1,128)S(1)}, u32[]{:S(2)}, u32[]{:S(2)}) async-start(s32[32,1,128]{2,1,0:T(1,128)} %broadcast_in_dim.62), calls=%async_computation | async-start | bytes 32768 | tf_op jit(solution)/shard_map/all_to_all | solution.py:19
  20.1 3.5 copy-start.2
  69.1 7.5 %copy-start.4 = (f32[3,3,128]{2,1,0:T(4,128)S(1)}, f32[3,3,128]{2,1,0:T(4,128)}, u32[]{:S(2)}) copy-start(f32[3,3,128]{2,1,0:T(4,128)} %param.13) | copy-start | bytes 13828
  72.3 6.4 %collective-permute-start = (bf16[3,32,2,128]{3,1,2,0:T(8,128)(2,1)S(1)}, bf16[3,32,2,128]{3,1,2,0:T(8,128)(2,1)S(1)}, u32[]{:S(2)}, u32[]{:S(2)}) collective-permute-start(bf16[3,32,2,128]{3,1,2,0:T(8,128)(2,1)S(1)} %copy.19), channel_id=1, source_target_pairs={{0,1},{1,2},{2,3},{4,5},{5,6},{6,7},{8,9},{9,10},{10,11},{12,13},{... | collective-permute-start | bytes 147464 | tf_op jit(solution)/shard_map/ppermute | solution.py:29
  88.0 2.7 copy-start.3
  91.1 7.5 %copy-start.5 = (bf16[8,128]{1,0:T(8,128)(2,1)S(1)}, bf16[8,128]{1,0:T(8,128)(2,1)}, u32[]{:S(2)}) copy-start(bf16[8,128]{1,0:T(8,128)(2,1)} %param.14) | copy-start | bytes 6148
  93.2 79.4 %collective-permute-start.1 = (bf16[32,127,128]{2,0,1:T(8,128)(2,1)}, bf16[32,127,128]{2,0,1:T(8,128)(2,1)}, u32[]{:S(2)}, u32[]{:S(2)}) collective-permute-start(bf16[32,127,128]{2,0,1:T(8,128)(2,1)} %copy.21), channel_id=1, source_target_pairs={{0,1},{1,2},{2,3},{4,5},{5,6},{6,7},{8,9},{9,10},{10,11},{12,13},{... | collective-permute-start | bytes 3121160 | tf_op jit(solution)/shard_map/ppermute | solution.py:29
  176.5 9.4 %copy-start.6 = (s32[1,128]{1,0:T(1,128)S(1)}, s32[1,128]{1,0:T(1,128)}, u32[]{:S(2)}) copy-start(s32[1,128]{1,0:T(1,128)} %param.9) | copy-start | bytes 1540
  179.5 34.4 %all-to-all-start.1 = ((bf16[32,128,128]{1,2,0:T(8,128)(2,1)}), bf16[32,128,128]{1,2,0:T(8,128)(2,1)S(1)}, u32[]{:S(2)}, u32[]{:S(2)}) async-start(bf16[32,128,128]{1,2,0:T(8,128)(2,1)} %fusion.16), calls=%async_computation.1 | async-start | bytes 2097152 | tf_op jit(solution)/shard_map/all_to_all | solution.py:73
  440.5 3.3 copy-start.1
Sparse Core Ops, SparseCore 0:
  10.5 275.6 all-gather.1
where the time goes:
time: 454 us; the launch traced here: 451 us
  local copies, waits for them, and re-layouts  133 us (29%)
  other arithmetic  120 us (26%)
  waiting for transfers between devices  99.6 us (22%)
  matrix products  57 us (13%)
  starting transfers between devices  26.9 us (6%)
  between operations  13.7 us (3%)
    add x32, other arithmetic, add_block(): return (partial_sum + block_out.astype(jnp.float32), None)  100 us
    gather x3, local copies, waits for them, and re-layouts, per_device(): jnp.take(conv_taps, jnp.clip(lag_grid, 0, TAPS - 1), axis=1)  73.6 us
    all_gather x1, waiting for transfers between devices, per_device(): weight_piece = lax.all_gather(out_proj, 'fsdp', axis=0, tiled=True)  72.4 us
    dot_general x32, matrix products, add_block(): jnp.dot(block_pair[0], block_pair[1], preferred_element_type=jnp.float32)  53.9 us
    gather x2, local copies, waits for them, and re-layouts, per_device(): projected = jnp.take(proj_table, all_ids, axis=1)  35.5 us
    all_to_all x1, waiting for transfers between devices, per_device(): lax.all_to_all(gated, 'fsdp', split_axis=0, concat_axis=2, tiled=True)[0]  22 us
    all_to_all x1, starting transfers between devices, from_everyone(): lax.all_to_all(jnp.broadcast_to(x[None], (peers, *x.shape)), axis, 0, 0,...  11.3 us
    ppermute x2, starting transfers between devices, from_behind(): return lax.ppermute(x, axis, pairs)  9.17 us
  transfers between devices with their start and end apart: 5, of which 4 were waited for; matrix products, arithmetic and copies ran while one was open for 33% of the time, Pallas kernels for 0%

commit v1 on v0

v1 whole, which is shorter than its diff:
```python
import jax
import jax.numpy as jnp
from jax import lax
from jax.experimental import pallas as pl
from jax.experimental.pallas import tpu as pltpu
from jax.sharding import PartitionSpec as P

GROUP = 16
TAPS = 128
SHORT = 3
VOCAB = 512
D = 4096
LEN = 512
CH = 32
CHUNKS = 4
CW = 512
F32 = jnp.float32
BF16 = jnp.bfloat16
MESH = pl.DeviceIdType.MESH

PA, PB, PH0, PH1, QA, QB, RA, RB = 0, 1, 2, 3, 4, 8, 12, 16
N_ROLES = 20


def dot_t(a, b):
    return lax.dot_general(a, b, (((1,), (1,)), ((), ())), preferred_element_type=F32)


def kernel(
    ids_ref, gain_ref, staps_ref, ctaps_ref, emb_ref, inp_ref, op_ref, out_ref,
    emb, inp, normed, sel, tab, ids, taps, toep, prod, qf, gsend, gath, lhs, wbuf,
    opp_s, opp_r, part, fin_s, fin_r, mine, resid, outb,
    ld_sem, wl_sem, id1_s, id1_r, id2_s, id2_r, w_s, w_r, g_s, g_r, gl_sem, b_s, b_r,
    o_s, o_r, f_s, f_r, m_s, m_r, out_sem,
):
    f = lax.axis_index("fsdp")
    c = lax.axis_index("ctx")
    xh, y, z = f // 16, (f // 4) % 4, f % 4
    xl, k = c // 2, c % 2
    x = xh * 2 + xl
    line = y * 4 + z

    def dev(xx, yy, zz, kk):
        return {"fsdp": (xx // 2) * 16 + yy * 4 + zz, "ctx": (xx % 2) * 2 + kk}

    def add(a, n):
        return (a + n) % 4

    def remote(src, dst, ssem, rsem, target):
        return pltpu.make_async_remote_copy(
            src_ref=src, dst_ref=dst, send_sem=ssem, recv_sem=rsem,
            device_id=target, device_id_type=MESH,
        )

    here = {"fsdp": f, "ctx": c}
    sent = []

    def send(src, dst, ssem, rsem, target):
        copy = remote(src, dst, ssem, rsem, target)
        copy.start()
        sent.append(copy)

    def arrived(dst, rsem):
        remote(dst, dst, rsem, rsem, here).wait_recv()

    line_peers = [(dx, dk) for dx in range(4) for dk in range(2) if (dx, dk) != (0, 0)]
    plane_peers = [(dy, dz) for dy in range(4) for dz in range(4) if (dy, dz) != (0, 0)]

    def line_dev(dx, dk):
        return dev(add(x, dx), y, z, (k + dk) % 2)

    def plane_dev(dy, dz):
        return dev(x, add(y, dy), add(z, dz), k)

    barrier = pltpu.get_barrier_semaphore()
    for dx, dk in line_peers:
        pl.semaphore_signal(barrier, inc=1, device_id=line_dev(dx, dk), device_id_type=MESH)
    for dy, dz in plane_peers:
        pl.semaphore_signal(barrier, inc=1, device_id=plane_dev(dy, dz), device_id_type=MESH)

    load_inp = pltpu.make_async_copy(inp_ref, inp, ld_sem.at[0])
    load_inp.start()
    load_emb = pltpu.make_async_copy(emb_ref, emb, ld_sem.at[1])
    load_emb.start()

    def w_source(j):
        cols = pl.multiple_of(k * (CHUNKS * CW) + j * CW, CW)
        return op_ref.at[pl.ds(pl.multiple_of(xl * 64, 64), 64), pl.ds(cols, CW)]

    own_w = []
    for j in range(CHUNKS):
        copy = pltpu.make_async_copy(w_source(j), wbuf.at[j, y, z], wl_sem.at[j])
        copy.start()
        own_w.append(copy)
    own_ids = pltpu.make_async_copy(ids_ref, ids.at[line, xh, c], ld_sem.at[2])
    own_ids.start()

    staps = jnp.concatenate(
        [staps_ref[j, :, :] for j in range(SHORT)] + [jnp.zeros((128 - 9, 128), F32)], axis=0
    )
    taps[...] = staps.T
    ch0 = pl.multiple_of(c * CH, CH)
    my_taps = taps[pl.ds(ch0, CH), :]
    tap_cols = [
        jnp.concatenate([my_taps[:, 3 * j + i : 3 * j + i + 1] for i in range(3)], axis=0)
        for j in range(SHORT)
    ]

    all_taps = ctaps_ref[...].astype(F32)
    rows8 = lax.broadcasted_iota(jnp.int32, (8, 128), 0)
    for g in range(2):
        row = jnp.sum(jnp.where(rows8 == 2 * c + g, all_taps, 0.0), axis=0, keepdims=True)
        base = jnp.concatenate([row, jnp.zeros((1, 384), F32)], axis=1)
        base = jnp.broadcast_to(base, (384, 512))
        band = pltpu.roll(base, 384, 1, stride=1, stride_axis=0)
        toep[g] = band[:, :256].astype(BF16)

    load_inp.wait()
    pick = (
        lax.broadcasted_iota(jnp.int32, (CH, 128), 1)
        == lax.broadcasted_iota(jnp.int32, (CH, 128), 0) + ch0
    )
    pick = jnp.where(pick, 1.0, 0.0).astype(BF16)
    for i in range(3):
        for d0 in range(0, D, 1024):
            sel[i * CH : (i + 1) * CH, d0 : d0 + 1024] = dot_t(
                pick, inp[i, d0 : d0 + 1024, :]
            ).astype(BF16)

    pl.semaphore_wait(barrier, len(line_peers) + len(plane_peers))

    for n, (dx, dk) in enumerate(line_peers):
        send(ids_ref, ids.at[line, xh, c], id1_s.at[n], id1_r.at[n], line_dev(dx, dk))

    def piece(j, p, q):
        return wbuf.at[j, p, q] if j % 2 == 0 else wbuf.at[j, q, p]

    def coords(j):
        return (y, z) if j % 2 == 0 else (z, y)

    def w_dev(j, dp, dq):
        return plane_dev(dp, dq) if j % 2 == 0 else plane_dev(dq, dp)

    def w_send(j, role, src, dst, dp, dq):
        send(src, dst, w_s.at[j, role], w_r.at[j, role], w_dev(j, dp, dq))

    lower, upper = pl.ds(0, 32), pl.ds(32, 32)

    def stage1(j):
        p, q = coords(j)
        src, dst = w_source(j), piece(j, p, q)
        w_send(j, PA, src, dst, 1, 0)
        w_send(j, PB, src, dst, 3, 0)
        w_send(j, QA, src, dst, 0, 1)
        w_send(j, QB, src, dst, 0, 3)

    def stage2(j):
        p, q = coords(j)
        a, b = piece(j, add(p, 3), q), piece(j, add(p, 1), q)
        arrived(a, w_r.at[j, PA])
        w_send(j, PH0, a.at[lower], a.at[lower], 1, 0)
        arrived(b, w_r.at[j, PB])
        w_send(j, PH1, b.at[upper], b.at[upper], 3, 0)
        w_send(j, QA + 1, a, a, 0, 1)
        w_send(j, QB + 1, a, a, 0, 3)
        w_send(j, QA + 2, b, b, 0, 1)
        w_send(j, QB + 2, b, b, 0, 3)

    def stage3(j):
        p, q = coords(j)
        a = piece(j, add(p, 2), q)
        arrived(a.at[lower], w_r.at[j, PH0])
        arrived(a.at[upper], w_r.at[j, PH1])
        w_send(j, QA + 3, a, a, 0, 1)
        w_send(j, QB + 3, a, a, 0, 3)

    order = (0, 3, 1, 2)

    def relay(j, i):
        p, q = coords(j)
        a = piece(j, add(p, order[i]), add(q, 3))
        b = piece(j, add(p, order[i]), add(q, 1))
        arrived(a, w_r.at[j, QA + i])
        w_send(j, RA + i, a.at[lower], a.at[lower], 0, 1)
        arrived(b, w_r.at[j, QB + i])
        w_send(j, RB + i, b.at[upper], b.at[upper], 0, 3)

    def stage4(j):
        for i in range(3):
            relay(j, i)

    def stage5(j):
        relay(j, 3)

    def stage6(j):
        p, q = coords(j)
        for i in range(4):
            a = piece(j, add(p, order[i]), add(q, 2))
            arrived(a.at[lower], w_r.at[j, RA + i])
            arrived(a.at[upper], w_r.at[j, RB + i])

    for j in range(CHUNKS):
        stage1(j)

    load_emb.wait()

    def norm_rows(b, carry):
        rows = pl.ds(pl.multiple_of(b * 32, 32), 32)
        values = emb[rows, :].astype(F32)
        inv = lax.rsqrt(jnp.mean(values * values, axis=-1, keepdims=True) + 1e-06)
        normed[rows, :] = (values * inv * gain_ref[...]).astype(BF16)
        return carry

    lax.fori_loop(0, 8, norm_rows, 0)

    own_ids.wait()
    for n, (dx, dk) in enumerate(line_peers):
        sx = add(x, 4 - dx)
        arrived(ids.at[line, sx // 2, (sx % 2) * 2 + (k + dk) % 2], id1_r.at[n])
    for n, (dy, dz) in enumerate(plane_peers):
        send(ids.at[line], ids.at[line], id2_s.at[n], id2_r.at[n], plane_dev(dy, dz))

    lax.fori_loop(8, 16, norm_rows, 0)

    table = dot_t(sel[...], normed[...]).astype(BF16)
    tab[0 : 3 * CH, :] = table[:, 0:256]
    tab[3 * CH : 6 * CH, :] = table[:, 256:512]

    own_hot = lax.broadcasted_iota(jnp.int32, (VOCAB, 128), 0) == ids_ref[...]
    own_hot = jnp.where(own_hot, 1.0, 0.0).astype(F32).T.astype(BF16)

    stage2(0)
    stage2(1)

    for n, (dy, dz) in enumerate(plane_peers):
        arrived(ids.at[add(y, 4 - dy) * 4 + add(z, 4 - dz)], id2_r.at[n])

    lane = lax.broadcasted_iota(jnp.int32, (3 * CH, LEN), 1)
    vocab = lax.broadcasted_iota(jnp.int32, (256, 128), 0)

    def mix_window(src_line, zz, h):
        hots, highs = [], []
        for b in range(4):
            row = ids[src_line, h, b]
            hots.append(jnp.where(vocab == (row & 255), 1.0, 0.0).astype(BF16))
            highs.append(row >> 8)
        hot = jnp.concatenate(hots, axis=1)
        high = jnp.concatenate(highs, axis=1)
        both = jnp.dot(tab[...], hot, preferred_element_type=F32)
        now = jnp.where(high == 1, both[3 * CH :], both[: 3 * CH])
        back1 = jnp.where(lane >= 1, pltpu.roll(now, 1, 1), 0.0)
        back2 = jnp.where(lane >= 2, pltpu.roll(now, 2, 1), 0.0)
        feat = tap_cols[0] * now + tap_cols[1] * back1 + tap_cols[2] * back2
        pr = (feat[CH : 2 * CH] * feat[2 * CH :]).astype(BF16)
        n = zz * 2 + h
        for g in range(2):
            rows = slice(g * GROUP, (g + 1) * GROUP)
            qf[g, n] = feat[rows]
            prod[g, n] = pr[rows]

    def mix_rows(yy):
        def one_line(zz, carry):
            for h in range(2):
                mix_window(yy * 4 + zz, zz, h)
            return carry

        lax.fori_loop(0, 4, one_line, 0)
        for g in range(2):
            p = prod[g].reshape(128, LEN)
            first = jnp.dot(p[:, :256], toep[g, 128:], preferred_element_type=F32)
            second = jnp.dot(p[:, 128:], toep[g], preferred_element_type=F32)
            filt = jnp.concatenate([first, second], axis=1).reshape(8, GROUP, LEN)
            for n in range(8):
                gsend[yy * 4 + n // 2, g * GROUP : (g + 1) * GROUP,
                      (n % 2) * LEN : (n % 2 + 1) * LEN] = (qf[g, n] * filt[n]).astype(BF16)

    my_rows = pl.ds(pl.multiple_of(k * CH, CH), CH)
    sib_rows = pl.ds(pl.multiple_of((1 - k) * CH, CH), CH)

    def scatter(dy):
        yy = add(y, dy)
        for dz in range(4):
            if (dy, dz) == (0, 0):
                continue
            n = dy * 4 + dz
            send(gsend.at[yy * 4 + add(z, dz)], gath.at[line, my_rows],
                 g_s.at[n], g_r.at[n], plane_dev(dy, dz))

    polls = {
        2: lambda: (stage2(2), stage2(3), stage3(0), stage3(1)),
        1: lambda: (stage4(0), stage4(1)),
        3: lambda: (stage3(2), stage3(3), stage5(0), stage5(1)),
        0: lambda: (stage4(2), stage4(3)),
    }
    for dy in (2, 1, 3, 0):
        mix_rows(add(y, dy))
        scatter(dy)
        polls[dy]()

    own_g = pltpu.make_async_copy(gsend.at[line], gath.at[line, my_rows], gl_sem)
    own_g.start()
    send(gsend.at[line], gath.at[line, my_rows], b_s.at[0], b_r.at[0], line_dev(0, 1))

    resid[...] = jnp.dot(own_hot, emb[...], preferred_element_type=F32).astype(BF16)

    for dy in (2, 1, 3, 0):
        for dz in range(4):
            if (dy, dz) == (0, 0):
                continue
            n = dy * 4 + dz
            there = gath.at[add(y, 4 - dy) * 4 + add(z, 4 - dz), my_rows]
            arrived(there, g_r.at[n])
            send(there, there, b_s.at[n], b_r.at[n], line_dev(0, 1))
    own_g.wait()
    stage5(2)
    stage5(3)
    for dy in (2, 1, 3, 0):
        sy = add(y, 4 - dy)
        for dz in range(4):
            arrived(gath.at[sy * 4 + add(z, 4 - dz), sib_rows], b_r.at[dy * 4 + dz])
        for pair in range(2):
            block = jnp.concatenate(
                [gath[sy * 4 + 2 * pair], gath[sy * 4 + 2 * pair + 1]], axis=0
            )
            cols = pl.multiple_of(sy * 256 + pair * 128, 128)
            lhs[:, pl.ds(cols, 128)] = block.T

    def block_of(dx):
        return pl.ds(pl.multiple_of(add(x, dx) * 256, 256), 256)

    def multiply(j):
        own_w[j].wait()
        stage6(j)

        def times(dx):
            w = wbuf[j].reshape(16 * 64, CW)
            return jnp.dot(lhs[block_of(dx), :], w, preferred_element_type=F32)

        far = times(2)
        opp_s[j, 0] = far[:, :256].astype(BF16)
        opp_s[j, 1] = far[:, 256:].astype(BF16)
        send(opp_s.at[j, 0], opp_r.at[j, 0], o_s.at[j, 0], o_r.at[j, 0], line_dev(1, 0))
        send(opp_s.at[j, 1], opp_r.at[j, 1], o_s.at[j, 1], o_r.at[j, 1], line_dev(3, 0))
        part[j, 0] = times(1)
        part[j, 1] = times(3)
        own = times(0).astype(BF16)
        for t in range(2):
            mine[t, j, k] = own[t * 128 : (t + 1) * 128]
        send(mine.at[1 - k, j, k], mine.at[1 - k, j, k], m_s.at[j], m_r.at[j], line_dev(0, 1))

    def pass_on(j):
        for side, dx in ((0, 1), (1, 3)):
            arrived(opp_r.at[j, side], o_r.at[j, side])
            half = slice(side * 256, (side + 1) * 256)
            rest = slice((1 - side) * 256, (2 - side) * 256)
            for t in range(2):
                rows = slice(t * 128, (t + 1) * 128)
                fin_s[j, side, t, :, half] = (
                    part[j, side, rows, half] + opp_r[j, side, rows, :].astype(F32)
                ).astype(BF16)
                fin_s[j, side, t, :, rest] = part[j, side, rows, rest].astype(BF16)
            for dk in range(2):
                t = (k + dk) % 2
                send(fin_s.at[j, side, t], fin_r.at[j, side, k],
                     f_s.at[j, side, dk], f_r.at[j, side, dk], line_dev(dx, dk))

    stores = []

    def finish(j):
        arrived(mine.at[k, j, 1 - k], m_r.at[j])
        for side in range(2):
            for dk in range(2):
                arrived(fin_r.at[j, side, (k + dk) % 2], f_r.at[j, side, dk])
        for h in range(2):
            cols = slice(h * CHUNKS * CW + j * CW, h * CHUNKS * CW + (j + 1) * CW)
            total = (
                fin_r[j, 0, h].astype(F32) + fin_r[j, 1, h].astype(F32)
                + mine[k, j, h].astype(F32) + resid[:, cols].astype(F32)
            )
            outb[:, cols] = total.astype(BF16)
            copy = pltpu.make_async_copy(
                outb.at[:, cols], out_ref.at[:, cols], out_sem.at[j, h]
            )
            copy.start()
            stores.append(copy)

    for j in range(CHUNKS):
        multiply(j)
        if j >= 1:
            pass_on(j - 1)
    pass_on(CHUNKS - 1)
    for j in range(CHUNKS):
        finish(j)

    for copy in stores:
        copy.wait()
    for copy in sent:
        copy.wait_send()


def per_device(token_ids, embedding, norm_gain, in_proj, short_taps, conv_taps, out_proj):
    vmem = pl.BlockSpec(memory_space=pltpu.VMEM)
    hbm = pl.BlockSpec(memory_space=pl.ANY)
    dma = pltpu.SemaphoreType.DMA
    out = pl.pallas_call(
        kernel,
        out_shape=jax.ShapeDtypeStruct((128, D), BF16),
        in_specs=[vmem, vmem, vmem, vmem, hbm, hbm, hbm],
        out_specs=hbm,
        scratch_shapes=[
            pltpu.VMEM((VOCAB, D), BF16),
            pltpu.VMEM((3, D, 128), BF16),
            pltpu.VMEM((VOCAB, D), BF16),
            pltpu.VMEM((3 * CH, D), BF16),
            pltpu.VMEM((6 * CH, 256), BF16),
            pltpu.VMEM((16, 2, 4, 1, 128), jnp.int32),
            pltpu.VMEM((128, 128), F32),
            pltpu.VMEM((2, 384, 256), BF16),
            pltpu.VMEM((2, 8, GROUP, LEN), BF16),
            pltpu.VMEM((2, 8, GROUP, LEN), F32),
            pltpu.VMEM((16, CH, 2 * LEN), BF16),
            pltpu.VMEM((16, 2 * CH, 2 * LEN), BF16),
            pltpu.VMEM((2 * LEN, 1024), BF16),
            pltpu.VMEM((CHUNKS, 4, 4, 64, CW), BF16),
            pltpu.VMEM((CHUNKS, 2, 256, 256), BF16),
            pltpu.VMEM((CHUNKS, 2, 256, 256), BF16),
            pltpu.VMEM((CHUNKS, 2, 256, CW), F32),
            pltpu.VMEM((CHUNKS, 2, 2, 128, CW), BF16),
            pltpu.VMEM((CHUNKS, 2, 2, 128, CW), BF16),
            pltpu.VMEM((2, CHUNKS, 2, 128, CW), BF16),
            pltpu.VMEM((128, D), BF16),
            pltpu.VMEM((128, D), BF16),
            dma((3,)), dma((CHUNKS,)), dma((7,)), dma((7,)), dma((15,)), dma((15,)),
            dma((CHUNKS, N_ROLES)), dma((CHUNKS, N_ROLES)), dma((16,)), dma((16,)), dma(()),
            dma((16,)), dma((16,)),
            dma((CHUNKS, 2)), dma((CHUNKS, 2)), dma((CHUNKS, 2, 2)), dma((CHUNKS, 2, 2)),
            dma((CHUNKS,)), dma((CHUNKS,)), dma((CHUNKS, 2)),
        ],
        compiler_params=pltpu.CompilerParams(
            collective_id=0, has_side_effects=True, vmem_limit_bytes=60 * 1024 * 1024
        ),
        name="mixer",
    )(token_ids, norm_gain.reshape(1, D), short_taps, conv_taps, embedding, in_proj, out_proj)
    return out[None]


def solution(mesh):
    return jax.shard_map(
        per_device,
        mesh=mesh,
        in_specs=(
            P("fsdp", "ctx"),
            P(),
            P(),
            P(None, None, "fsdp"),
            P(None, None, "fsdp"),
            P("fsdp", None),
            P("fsdp", None),
        ),
        out_specs=P("fsdp", "ctx", None),
        check_vma=False,
    )
```

time: 454 us -> 89.6 us (0.20)
  local copies, waits for them, and re-layouts: 133 us -> 2.29 us
  other arithmetic: 120 us -> 0 us
  waiting for transfers between devices: 99.6 us -> 0 us
  Pallas kernels: 0 us -> 87.2 us
  matrix products: 57 us -> 0 us
  starting transfers between devices: 26.9 us -> 0 us
  between operations: 13.7 us -> 0.01 us
    gather x6 -> x0, local copies, waits for them, and re-layouts: 115 us -> none  [the longest x3 73.6 us: per_device(): jnp.take(conv_taps, jnp.clip(lag_grid, 0, TAPS - 1), axis=1)]
    add x34 -> x0, other arithmetic: 107 us -> none  [the longest x32 100 us: add_block(): return (partial_sum + block_out.astype(jnp.float32), None)]
    pallas_call x0 -> x1, Pallas kernels: none -> 87.2 us  [per_device(): pl.pallas_call(kernel, out_shape=jax.ShapeDtypeStruct((128, D), BF16), in...]
    all_gather x1 -> x0, waiting for transfers between devices: 72.4 us -> none  [per_device(): weight_piece = lax.all_gather(out_proj, 'fsdp', axis=0, tiled=True)]
    dot_general x34 -> x0, matrix products: 57 us -> none  [the longest x32 53.9 us: add_block(): jnp.dot(block_pair[0], block_pair[1], preferred_element_type=jnp.float32)]
    all_to_all x2 -> x0, waiting for transfers between devices: 24.4 us -> none  [the longest x1 22 us: per_device(): lax.all_to_all(gated, 'fsdp', split_axis=0, concat_axis=2, tiled=True)[0]]
    all_to_all x2 -> x0, starting transfers between devices: 17.8 us -> none  [the longest x1 11.3 us: from_everyone(): lax.all_to_all(jnp.broadcast_to(x[None], (peers, *x.shape)), axis, 0, 0,...]
    ppermute x2 -> x0, starting transfers between devices: 9.17 us -> none  [from_behind(): return lax.ppermute(x, axis, pairs)]
  transfers between devices with their start and end apart: 5 -> 0, of which waited for: 4 -> 0; matrix products, arithmetic and copies ran while one was open for 33% -> 0% of each run, Pallas kernels for 0% -> 0%
where the time goes in v1:
time: 89.6 us; the launch traced here: 89.5 us
  Pallas kernels  87.2 us (97%)
  local copies, waits for them, and re-layouts  2.29 us (3%)
    pallas_call x1, Pallas kernels, per_device(): pl.pallas_call(kernel, out_shape=jax.ShapeDtypeStruct((128, D), BF16), in...  87.2 us
    unnamed x1, local copies, waits for them, and re-layouts  2.29 us

profile of v1, /device:TPU:1, one launch (start us, length us, event | category | flops | bytes accessed | tf_op | source)
XLA Modules:
  0.0 89.5 jit_solution(4911372198181224629)
XLA Ops:
  0.0 87.2 %mixer.1 = bf16[128,4096]{1,0:T(8,128)(2,1)} custom-call(s32[1,128]{1,0:T(1,128)} %ids_ref.1, f32[1,4096]{1,0:T(1,128)} %bitcast.3, f32[3,3,128]{2,1,0:T(4,128)} %staps_ref.1, bf16[8,128]{1,0:T(8,128)(2,1)} %ctaps_ref.1, bf16[512,4096]{1,0:T(8,128)(2,1)} %emb_ref.1, bf16[3,4096,128]{2,1,0:T(8,128)(2,1)} %inp_ref.1, bf16[128,4096]{1,0:T(8,128)(2,1)} %op_ref.1), custom_call_target="tpu_custom_call" | custom-call | tf_op jit(solution)/shard_map/mixer/pallas_call | solution.py:405
  87.2 2.3 %copy.9 = bf16[1,128,4096]{2,1,0:T(8,128)(2,1)} copy(bf16[1,128,4096]{2,1,0:T(8,128)(2,1)} %bitcast.2) | data formatting | bytes 2097152

commit v2 on v1

v2 whole, which is shorter than its diff:
```python
import jax
import jax.numpy as jnp
from jax import lax
from jax.experimental import pallas as pl
from jax.experimental.pallas import tpu as pltpu
from jax.sharding import PartitionSpec as P

GROUP = 16
TAPS = 128
SHORT = 3
VOCAB = 512
D = 4096
LEN = 512
CH = 32
CHUNKS = 4
CW = 512
F32 = jnp.float32
BF16 = jnp.bfloat16
MESH = pl.DeviceIdType.MESH

PA, PB, PH0, PH1, QA, QB, RA, RB = 0, 1, 2, 3, 4, 8, 12, 16
ROUND = {PA: 0, PB: 0, PH0: 1, PH1: 1, QA: 2, QA + 1: 2, QA + 2: 2, QA + 3: 3,
         QB: 2, QB + 1: 2, QB + 2: 2, QB + 3: 3, **{RA + i: 4 for i in range(8)}}
N_ONE = 13


def dot_t(a, b):
    return lax.dot_general(a, b, (((1,), (1,)), ((), ())), preferred_element_type=F32)


def kernel(
    ids_ref, gain_ref, staps_ref, ctaps_ref, emb_ref, inp_ref, op_ref, out_ref,
    emb, inp, normed, sel, tab, ids, taps, tapb, toep, prod, qf, gsend, gath, lhs, wbuf,
    opp_s, opp_r, part, fin_s, fin_r, mine, resid, outb,
    ld_sem, one_sem, w_r, g_r, b_r, o_r, f_r, m_r,
):
    wl_sem, gl_sem, out_sem, is_sem, ir_sem, i_s, i_r, w_s, g_s, b_s, o_s, f_s, m_s = (
        one_sem.at[i] for i in range(N_ONE)
    )
    f = lax.axis_index("fsdp")
    c = lax.axis_index("ctx")
    xh, y, z = f // 16, (f // 4) % 4, f % 4
    xl, k = c // 2, c % 2
    x = xh * 2 + xl
    line = y * 4 + z

    def dev(xx, yy, zz, kk):
        return {"fsdp": (xx // 2) * 16 + yy * 4 + zz, "ctx": (xx % 2) * 2 + kk}

    def add(a, n):
        return (a + n) % 4

    def remote(src, dst, ssem, rsem, target):
        return pltpu.make_async_remote_copy(
            src_ref=src, dst_ref=dst, send_sem=ssem, recv_sem=rsem,
            device_id=target, device_id_type=MESH,
        )

    here = {"fsdp": f, "ctx": c}
    def send(src, dst, ssem, rsem, target):
        remote(src, dst, ssem, rsem, target).start()

    def arrived(dst, rsem):
        remote(dst, dst, rsem, rsem, here).wait_recv()

    def all_sent(src, ssem):
        remote(src, src, ssem, ssem, here).wait_send()

    def line_dev(dx, dk):
        return dev(add(x, dx), y, z, (k + dk) % 2)

    def plane_dev(dy, dz):
        return dev(x, add(y, dy), add(z, dz), k)

    chip = line * 4 + x

    load_inp = pltpu.make_async_copy(inp_ref, inp, ld_sem.at[0])
    load_inp.start()
    load_emb = pltpu.make_async_copy(emb_ref, emb, ld_sem.at[1])
    load_emb.start()

    def w_source(j):
        cols = pl.multiple_of(k * (CHUNKS * CW) + j * CW, CW)
        return op_ref.at[pl.ds(pl.multiple_of(xl * 64, 64), 64), pl.ds(cols, CW)]

    for j in range(CHUNKS):
        pltpu.make_async_copy(w_source(j), wbuf.at[j * 16 + line], wl_sem).start()
    own_ids = pltpu.make_async_copy(ids_ref, ids.at[chip, k], ld_sem.at[2])
    own_ids.start()

    xs = [add(x, i) for i in range(4)]
    ctxs = [(xx % 2) * 2 + k for xx in xs]
    fsdps = [(xx // 2) * 16 for xx in xs]
    rows = [add(y, i) * 4 for i in range(4)]
    cols = [add(z, i) for i in range(4)]
    chips = [(dx, dy, dz) for dy in range(4) for dz in range(4) for dx in range(4)][1:]

    def chip_dev(dx, dy, dz):
        return {"fsdp": fsdps[dx] + rows[dy] + cols[dz], "ctx": ctxs[dx]}

    barrier = pltpu.get_barrier_semaphore()
    for dx in (0, 1, 3):
        pl.semaphore_signal(barrier, inc=1, device_id=line_dev(dx, 1), device_id_type=MESH)
    for d in chips:
        pl.semaphore_signal(barrier, inc=1, device_id=chip_dev(*d), device_id_type=MESH)
    staps = jnp.concatenate(
        [staps_ref[j, :, :] for j in range(SHORT)] + [jnp.zeros((128 - 9, 128), F32)], axis=0
    )
    taps[...] = staps.T
    ch0 = pl.multiple_of(c * CH, CH)
    my_taps = taps[pl.ds(ch0, CH), :]
    for j in range(SHORT):
        for i in range(3):
            tapb[j, i * CH : (i + 1) * CH, :] = jnp.broadcast_to(
                my_taps[:, 3 * j + i : 3 * j + i + 1], (CH, 128)
            )

    all_taps = ctaps_ref[...].astype(F32)
    rows8 = lax.broadcasted_iota(jnp.int32, (8, 128), 0)
    for g in range(2):
        row = jnp.sum(jnp.where(rows8 == 2 * c + g, all_taps, 0.0), axis=0, keepdims=True)
        base = jnp.concatenate([row, jnp.zeros((1, 384), F32)], axis=1)
        base = jnp.broadcast_to(base, (384, 512))
        band = pltpu.roll(base, 384, 1, stride=1, stride_axis=0)
        toep[g] = band[:, :256].astype(BF16)

    load_inp.wait()
    pick = (
        lax.broadcasted_iota(jnp.int32, (CH, 128), 1)
        == lax.broadcasted_iota(jnp.int32, (CH, 128), 0) + ch0
    )
    pick = jnp.where(pick, 1.0, 0.0).astype(BF16)
    for i in range(3):
        for d0 in range(0, D, 1024):
            sel[i * CH : (i + 1) * CH, d0 : d0 + 1024] = dot_t(
                pick, inp[i, d0 : d0 + 1024, :]
            ).astype(BF16)
    pl.semaphore_wait(barrier, 66)
    own_ids.wait()
    send(ids_ref, ids.at[chip, k], is_sem, ir_sem, line_dev(0, 1))

    def piece(j, p, q):
        return wbuf.at[j * 16 + (p * 4 + q if j % 2 == 0 else q * 4 + p)]

    def coords(j):
        return (y, z) if j % 2 == 0 else (z, y)

    def w_dev(j, dp, dq):
        return plane_dev(dp, dq) if j % 2 == 0 else plane_dev(dq, dp)

    def w_send(j, role, src, dst, dp, dq):
        send(src, dst, w_s, w_r.at[j, ROUND[role]], w_dev(j, dp, dq))

    def w_arrived(j, n, pieces):
        arrived(wbuf.at[pl.ds(j * 16, pieces)], w_r.at[j, n])

    lower, upper = pl.ds(0, 32), pl.ds(32, 32)

    def stage1(j):
        p, q = coords(j)
        src, dst = w_source(j), piece(j, p, q)
        w_send(j, PA, src, dst, 1, 0)
        w_send(j, PB, src, dst, 3, 0)
        w_send(j, QA, src, dst, 0, 1)
        w_send(j, QB, src, dst, 0, 3)

    def stage2(j):
        p, q = coords(j)
        a, b = piece(j, add(p, 3), q), piece(j, add(p, 1), q)
        w_arrived(j, 0, 2)
        w_send(j, PH0, a.at[lower], a.at[lower], 1, 0)
        w_send(j, PH1, b.at[upper], b.at[upper], 3, 0)
        w_send(j, QA + 1, a, a, 0, 1)
        w_send(j, QB + 1, a, a, 0, 3)
        w_send(j, QA + 2, b, b, 0, 1)
        w_send(j, QB + 2, b, b, 0, 3)

    def stage3(j):
        p, q = coords(j)
        a = piece(j, add(p, 2), q)
        w_arrived(j, 1, 1)
        w_send(j, QA + 3, a, a, 0, 1)
        w_send(j, QB + 3, a, a, 0, 3)

    order = (0, 3, 1, 2)

    def relay(j, i):
        p, q = coords(j)
        a = piece(j, add(p, order[i]), add(q, 3))
        b = piece(j, add(p, order[i]), add(q, 1))
        w_send(j, RA + i, a.at[lower], a.at[lower], 0, 1)
        w_send(j, RB + i, b.at[upper], b.at[upper], 0, 3)

    def stage4(j):
        w_arrived(j, 2, 6)
        for i in range(3):
            relay(j, i)

    def stage5(j):
        w_arrived(j, 3, 2)
        relay(j, 3)

    def stage6(j):
        w_arrived(j, 4, 4)
    stage1(0)
    stage1(1)
    load_emb.wait()

    def norm_rows(b, carry):
        rows = pl.ds(pl.multiple_of(b * 32, 32), 32)
        values = emb[rows, :].astype(F32)
        inv = lax.rsqrt(jnp.mean(values * values, axis=-1, keepdims=True) + 1e-06)
        normed[rows, :] = (values * inv * gain_ref[...]).astype(BF16)
        return carry
    lax.fori_loop(0, 4, norm_rows, 0)
    arrived(ids.at[chip, 1 - k], ir_sem)
    for d in chips:
        send(ids.at[chip], ids.at[chip], i_s, i_r, chip_dev(*d))
    lax.fori_loop(4, 16, norm_rows, 0)
    table = dot_t(sel[...], normed[...]).astype(BF16)
    tab[0 : 3 * CH, :] = table[:, 0:256]
    tab[3 * CH : 6 * CH, :] = table[:, 256:512]
    stage2(0)
    stage2(1)

    own_hot = lax.broadcasted_iota(jnp.int32, (VOCAB, 128), 0) == ids_ref[...]
    own_hot = jnp.where(own_hot, 1.0, 0.0).astype(F32).T.astype(BF16)
    resid[...] = jnp.dot(own_hot, emb[...], preferred_element_type=F32).astype(BF16)
    arrived(ids.at[pl.ds(0, 63)], i_r)

    lane = lax.broadcasted_iota(jnp.int32, (3 * CH, 128), 1).astype(F32).astype(BF16)
    not_first, not_two = lane >= 1, lane >= 2
    none = jnp.zeros((3 * CH, 128), BF16)
    vocab = lax.broadcasted_iota(jnp.int32, (256, 128), 0).astype(F32).astype(BF16)
    one, zero = jnp.ones((256, 128), BF16), jnp.zeros((256, 128), BF16)

    def mix_window(src_line, zz, h):
        hots, highs = [], []
        for b in range(4):
            row = ids[src_line * 4 + h * 2 + b // 2, b % 2]
            low = jnp.broadcast_to((row & 255).astype(F32).astype(BF16), (256, 128))
            hots.append(jnp.where(vocab == low, one, zero))
            highs.append(row >> 8)
        both = jnp.dot(tab[...], jnp.concatenate(hots, axis=1), preferred_element_type=F32)
        n = zz * 2 + h
        last1 = last2 = none
        for b in range(4):
            cols = slice(b * 128, (b + 1) * 128)
            now = jnp.where(highs[b] == 1, both[3 * CH :, cols], both[: 3 * CH, cols])
            packed = now.astype(BF16)
            roll1, roll2 = pltpu.roll(packed, 1, 1), pltpu.roll(packed, 2, 1)
            back1 = jnp.where(not_first, roll1, last1)
            back2 = jnp.where(not_two, roll2, last2)
            last1, last2 = roll1, roll2
            feat = tapb[0] * now + tapb[1] * back1.astype(F32) + tapb[2] * back2.astype(F32)
            pr = (feat[CH : 2 * CH] * feat[2 * CH :]).astype(BF16)
            for g in range(2):
                rows = slice(g * GROUP, (g + 1) * GROUP)
                qf[g, n, :, cols] = feat[rows]
                prod[g, n, :, cols] = pr[rows]

    def mix_rows(yy):
        def one_line(zz, carry):
            for h in range(2):
                mix_window(yy * 4 + zz, zz, h)
            return carry

        lax.fori_loop(0, 4, one_line, 0)
        for g in range(2):
            p = prod[g].reshape(128, LEN)
            first = jnp.dot(p[:, :256], toep[g, 128:], preferred_element_type=F32)
            second = jnp.dot(p[:, 128:], toep[g], preferred_element_type=F32)
            filt = jnp.concatenate([first, second], axis=1).reshape(8, GROUP, LEN)
            for n in range(8):
                gated = (qf[g, n] * filt[n]).astype(BF16)
                for b in range(4):
                    lanes = ((b % 2) * 4 + (n % 2) * 2 + b // 2) * 128
                    gsend[yy * 4 + n // 2, g * GROUP : (g + 1) * GROUP, lanes : lanes + 128] = (
                        gated[:, b * 128 : (b + 1) * 128]
                    )

    my_rows = pl.ds(pl.multiple_of(k * CH, CH), CH)
    sib_rows = pl.ds(pl.multiple_of((1 - k) * CH, CH), CH)

    half_lanes = (pl.ds(0, LEN), pl.ds(LEN, LEN))

    def scatter(dy, t):
        yy = add(y, dy)
        for dz in range(4):
            if (dy, dz) == (0, 0):
                continue
            send(gsend.at[yy * 4 + add(z, dz), :, half_lanes[t]],
                 gath.at[line, my_rows, half_lanes[t]],
                 g_s, g_r.at[t, dy], plane_dev(dy, dz))

    polls = {2: lambda: (stage3(0),stage3(1),),1: lambda: (stage4(0),stage4(1),),3: lambda: (stage5(0),stage5(1),),0: lambda: (stage1(2),stage1(3),)}
    for dy in (2, 1, 3, 0):
        mix_rows(add(y, dy))
        scatter(dy, 0)
        polls[dy]()

    own_g = pltpu.make_async_copy(gsend.at[line], gath.at[line, my_rows], gl_sem)
    own_g.start()

    def row_of(dy):
        return pl.ds(pl.multiple_of(add(y, 4 - dy) * 4, 4), 4)

    def hand_over(t):
        lanes = half_lanes[t]
        for dy in (2, 1, 3, 0):
            arrived(gath.at[pl.ds(0, 4 if dy else 3), my_rows, lanes], g_r.at[t, dy])
            if t == 0 and dy == 0:
                own_g.wait()
            there = gath.at[row_of(dy), my_rows, lanes]
            send(there, there, b_s, b_r.at[t, dy], line_dev(0, 1))

    def fill_lhs(t):
        lanes = half_lanes[t]
        for dy in (2, 1, 3, 0):
            sy = add(y, 4 - dy)
            arrived(gath.at[row_of(dy), sib_rows, lanes], b_r.at[t, dy])
            for pair in range(2):
                block = jnp.concatenate(
                    [gath[sy * 4 + 2 * pair, :, lanes], gath[sy * 4 + 2 * pair + 1, :, lanes]],
                    axis=0,
                )
                cols = pl.multiple_of(sy * 256 + pair * 128, 128)
                lhs[t * LEN : (t + 1) * LEN, pl.ds(cols, 128)] = block.T

    def w_ready(j):
        stage6(j)

    def multiply(t, j):

        def times(dx):
            w = wbuf[j * 16 : (j + 1) * 16].reshape(16 * 64, CW)
            rows = pl.ds(pl.multiple_of(t * LEN + add(x, dx) * 128, 128), 128)
            return jnp.dot(lhs[rows, :], w, preferred_element_type=F32)

        far = times(2).astype(BF16)
        for side, dx in ((0, 1), (1, 3)):
            opp_s[j, t, side] = far[:, side * 256 : (side + 1) * 256]
            send(opp_s.at[j, t, side], opp_r.at[j, t, side],
                 o_s, o_r.at[j, t], line_dev(dx, 0))
        part[j, t, 0] = times(1)
        part[j, t, 1] = times(3)
        mine[t, j, k] = times(0).astype(BF16)
        if t == 1:
            send(mine.at[1 - k, j, k], mine.at[1 - k, j, k], m_s, m_r.at[j], line_dev(0, 1))

    def pass_on(t, j):
        arrived(opp_r.at[j, t], o_r.at[j, t])
        for side, dx in ((0, 1), (1, 3)):
            half = slice(side * 256, (side + 1) * 256)
            rest = slice((1 - side) * 256, (2 - side) * 256)
            fin_s[j, t, side, :, rest] = part[j, t, side, :, rest].astype(BF16)
            fin_s[j, t, side, :, half] = (
                part[j, t, side, :, half] + opp_r[j, t, side].astype(F32)
            ).astype(BF16)
            send(fin_s.at[j, t, side], fin_r.at[j, side, k],
                 f_s, f_r.at[j], dev(add(x, dx), y, z, t))

    def finish(j):
        arrived(mine.at[k, j, 1 - k], m_r.at[j])
        arrived(fin_r.at[j], f_r.at[j])
        for h in range(2):
            cols = slice(h * CHUNKS * CW + j * CW, h * CHUNKS * CW + (j + 1) * CW)
            total = (
                fin_r[j, 0, h].astype(F32) + fin_r[j, 1, h].astype(F32)
                + mine[k, j, h].astype(F32) + resid[:, cols].astype(F32)
            )
            outb[:, cols] = total.astype(BF16)
            pltpu.make_async_copy(outb.at[:, cols], out_ref.at[:, cols], out_sem).start()
    hand_over(0)
    for dy in (2, 1, 3, 0):
        scatter(dy, 1)
    fill_lhs(0)
    pltpu.make_async_copy(wbuf.at[pl.ds(0, CHUNKS)], wbuf.at[pl.ds(0, CHUNKS)], wl_sem).wait()
    w_ready(0)
    multiply(0, 0)
    w_ready(1)
    multiply(0, 1)
    pass_on(0, 0)
    pass_on(0, 1)
    hand_over(1)
    stage2(2)
    stage2(3)
    fill_lhs(1)
    multiply(1, 0)
    multiply(1, 1)
    stage3(2)
    stage3(3)
    pass_on(1, 0)
    stage4(2)
    stage4(3)
    pass_on(1, 1)
    stage5(2)
    stage5(3)
    w_ready(2)
    multiply(0, 2)
    multiply(1, 2)
    w_ready(3)
    multiply(0, 3)
    pass_on(0, 2)
    multiply(1, 3)
    pass_on(1, 2)
    pass_on(0, 3)
    pass_on(1, 3)
    for j in range(CHUNKS):
        finish(j)
    pltpu.make_async_copy(outb, out_ref, out_sem).wait()
    all_sent(ids.at[chip, k], is_sem)
    all_sent(ids.at[pl.ds(0, 63)], i_s)
    all_sent(wbuf.at[pl.ds(0, 15 * CHUNKS)], w_s)
    all_sent(gath.at[pl.ds(0, 15), pl.ds(0, CH), :], g_s)
    all_sent(gath.at[:, pl.ds(0, CH), :], b_s)
    all_sent(opp_s, o_s)
    all_sent(fin_s, f_s)
    all_sent(mine.at[0, :, 0], m_s)


def per_device(token_ids, embedding, norm_gain, in_proj, short_taps, conv_taps, out_proj):
    vmem = pl.BlockSpec(memory_space=pltpu.VMEM)
    hbm = pl.BlockSpec(memory_space=pl.ANY)
    dma = pltpu.SemaphoreType.DMA
    out = pl.pallas_call(
        kernel,
        out_shape=jax.ShapeDtypeStruct((128, D), BF16),
        in_specs=[vmem, vmem, vmem, vmem, hbm, hbm, hbm],
        out_specs=hbm,
        scratch_shapes=[
            pltpu.VMEM((VOCAB, D), BF16),
            pltpu.VMEM((3, D, 128), BF16),
            pltpu.VMEM((VOCAB, D), BF16),
            pltpu.VMEM((3 * CH, D), BF16),
            pltpu.VMEM((6 * CH, 256), BF16),
            pltpu.VMEM((64, 2, 1, 128), jnp.int32),
            pltpu.VMEM((128, 128), F32),
            pltpu.VMEM((SHORT, 3 * CH, 128), F32),
            pltpu.VMEM((2, 384, 256), BF16),
            pltpu.VMEM((2, 8, GROUP, LEN), BF16),
            pltpu.VMEM((2, 8, GROUP, LEN), F32),
            pltpu.VMEM((16, CH, 2 * LEN), BF16),
            pltpu.VMEM((16, 2 * CH, 2 * LEN), BF16),
            pltpu.VMEM((2 * LEN, 1024), BF16),
            pltpu.VMEM((CHUNKS * 16, 64, CW), BF16),
            pltpu.VMEM((CHUNKS, 2, 2, 128, 256), BF16),
            pltpu.VMEM((CHUNKS, 2, 2, 128, 256), BF16),
            pltpu.VMEM((CHUNKS, 2, 2, 128, CW), F32),
            pltpu.VMEM((CHUNKS, 2, 2, 128, CW), BF16),
            pltpu.VMEM((CHUNKS, 2, 2, 128, CW), BF16),
            pltpu.VMEM((2, CHUNKS, 2, 128, CW), BF16),
            pltpu.VMEM((128, D), BF16),
            pltpu.VMEM((128, D), BF16),
            dma((3,)), dma((N_ONE,)), dma((CHUNKS, 5)), dma((2, 4)), dma((2, 4)),
            dma((CHUNKS, 2)), dma((CHUNKS,)), dma((CHUNKS,)),
        ],
        compiler_params=pltpu.CompilerParams(
            collective_id=0, has_side_effects=True, vmem_limit_bytes=60 * 1024 * 1024
        ),
        name="mixer",
    )(token_ids, norm_gain.reshape(1, D), short_taps, conv_taps, embedding, in_proj, out_proj)
    return out[None]


def solution(mesh):
    return jax.shard_map(
        per_device,
        mesh=mesh,
        in_specs=(
            P("fsdp", "ctx"),
            P(),
            P(),
            P(None, None, "fsdp"),
            P(None, None, "fsdp"),
            P("fsdp", None),
            P("fsdp", None),
        ),
        out_specs=P("fsdp", "ctx", None),
        check_vma=False,
    )
```

time: 89.6 us -> 77.5 us (0.86)
  Pallas kernels: 87.2 us -> 75 us
    pallas_call x1, Pallas kernels: 87.2 us -> 75 us  [per_device(): pl.pallas_call(kernel, out_shape=jax.ShapeDtypeStruct((128, D), BF16), in...]
where the time goes in v2:
time: 77.5 us; the launch traced here: 77.3 us
  Pallas kernels  75 us (97%)
  local copies, waits for them, and re-layouts  2.29 us (3%)
    pallas_call x1, Pallas kernels, per_device(): pl.pallas_call(kernel, out_shape=jax.ShapeDtypeStruct((128, D), BF16), in...  75 us
    unnamed x1, local copies, waits for them, and re-layouts  2.29 us

profile of v2, /device:TPU:1, one launch (start us, length us, event | category | flops | bytes accessed | tf_op | source)
XLA Modules:
  0.0 77.3 jit_solution(17089397831414242604)
XLA Ops:
  0.0 75.0 %mixer.1 = bf16[128,4096]{1,0:T(8,128)(2,1)} custom-call(s32[1,128]{1,0:T(1,128)} %ids_ref.1, f32[1,4096]{1,0:T(1,128)} %bitcast.3, f32[3,3,128]{2,1,0:T(4,128)} %staps_ref.1, bf16[8,128]{1,0:T(8,128)(2,1)} %ctaps_ref.1, bf16[512,4096]{1,0:T(8,128)(2,1)} %emb_ref.1, bf16[3,4096,128]{2,1,0:T(8,128)(2,1)} %inp_ref.1, bf16[128,4096]{1,0:T(8,128)(2,1)} %op_ref.1), custom_call_target="tpu_custom_call" | custom-call | tf_op jit(solution)/shard_map/mixer/pallas_call | solution.py:426
  75.0 2.3 %copy.9 = bf16[1,128,4096]{2,1,0:T(8,128)(2,1)} copy(bf16[1,128,4096]{2,1,0:T(8,128)(2,1)} %bitcast.2) | data formatting | bytes 2097152

commit v3 on v2

--- a/solution.py
+++ b/solution.py
@@ -21,7 +21,7 @@
 PA, PB, PH0, PH1, QA, QB, RA, RB = 0, 1, 2, 3, 4, 8, 12, 16
 ROUND = {PA: 0, PB: 0, PH0: 1, PH1: 1, QA: 2, QA + 1: 2, QA + 2: 2, QA + 3: 3,
          QB: 2, QB + 1: 2, QB + 2: 2, QB + 3: 3, **{RA + i: 4 for i in range(8)}}
-N_ONE = 13
+N_ONE = 12
 
 
 def dot_t(a, b):
@@ -29,12 +29,13 @@
 
 
 def kernel(
-    ids_ref, gain_ref, staps_ref, ctaps_ref, emb_ref, inp_ref, op_ref, out_ref,
+    ids_in, gain_in, staps_in, ctaps_in, emb_ref, inp_ref, op_ref, out_ref,
+    ids_ref, gain_ref, staps_ref, ctaps_ref,
     emb, inp, normed, sel, tab, ids, taps, tapb, toep, prod, qf, gsend, gath, lhs, wbuf,
-    opp_s, opp_r, part, fin_s, fin_r, mine, resid, outb,
+    opp_s, opp_r, part, fin_s, fin_r, mine, resid,
     ld_sem, one_sem, w_r, g_r, b_r, o_r, f_r, m_r,
 ):
-    wl_sem, gl_sem, out_sem, is_sem, ir_sem, i_s, i_r, w_s, g_s, b_s, o_s, f_s, m_s = (
+    wl_sem, gl_sem, is_sem, ir_sem, i_s, i_r, w_s, g_s, b_s, o_s, f_s, m_s = (
         one_sem.at[i] for i in range(N_ONE)
     )
     f = lax.axis_index("fsdp")
@@ -74,6 +75,12 @@
 
     chip = line * 4 + x
 
+    small = []
+    for i, (src, dst) in enumerate((
+        (ids_in, ids_ref), (staps_in, staps_ref), (ctaps_in, ctaps_ref), (gain_in, gain_ref)
+    )):
+        small.append(pltpu.make_async_copy(src, dst, ld_sem.at[2 + i]))
+        small[-1].start()
     load_inp = pltpu.make_async_copy(inp_ref, inp, ld_sem.at[0])
     load_inp.start()
     load_emb = pltpu.make_async_copy(emb_ref, emb, ld_sem.at[1])
@@ -85,7 +92,7 @@
 
     for j in range(CHUNKS):
         pltpu.make_async_copy(w_source(j), wbuf.at[j * 16 + line], wl_sem).start()
-    own_ids = pltpu.make_async_copy(ids_ref, ids.at[chip, k], ld_sem.at[2])
+    own_ids = pltpu.make_async_copy(ids_in, ids.at[chip, k], ld_sem.at[6])
     own_ids.start()
 
     xs = [add(x, i) for i in range(4)]
@@ -103,6 +110,8 @@
         pl.semaphore_signal(barrier, inc=1, device_id=line_dev(dx, 1), device_id_type=MESH)
     for d in chips:
         pl.semaphore_signal(barrier, inc=1, device_id=chip_dev(*d), device_id_type=MESH)
+    for copy in small:
+        copy.wait()
     staps = jnp.concatenate(
         [staps_ref[j, :, :] for j in range(SHORT)] + [jnp.zeros((128 - 9, 128), F32)], axis=0
     )
@@ -293,7 +302,7 @@
                  gath.at[line, my_rows, half_lanes[t]],
                  g_s, g_r.at[t, dy], plane_dev(dy, dz))
 
-    polls = {2: lambda: (stage3(0),stage3(1),),1: lambda: (stage4(0),stage4(1),),3: lambda: (stage5(0),stage5(1),),0: lambda: (stage1(2),stage1(3),)}
+    polls = {2: lambda: (None,),1: lambda: (stage3(0),stage3(1),),3: lambda: (stage4(0),stage4(1),),0: lambda: (stage5(0),stage5(1),)}
     for dy in (2, 1, 3, 0):
         mix_rows(add(y, dy))
         scatter(dy, 0)
@@ -369,11 +378,12 @@
                 fin_r[j, 0, h].astype(F32) + fin_r[j, 1, h].astype(F32)
                 + mine[k, j, h].astype(F32) + resid[:, cols].astype(F32)
             )
-            outb[:, cols] = total.astype(BF16)
-            pltpu.make_async_copy(outb.at[:, cols], out_ref.at[:, cols], out_sem).start()
+            out_ref[:, cols] = total.astype(BF16)
     hand_over(0)
     for dy in (2, 1, 3, 0):
         scatter(dy, 1)
+    stage1(2)
+    stage1(3)
     fill_lhs(0)
     pltpu.make_async_copy(wbuf.at[pl.ds(0, CHUNKS)], wbuf.at[pl.ds(0, CHUNKS)], wl_sem).wait()
     w_ready(0)
@@ -408,7 +418,6 @@
     pass_on(1, 3)
     for j in range(CHUNKS):
         finish(j)
-    pltpu.make_async_copy(outb, out_ref, out_sem).wait()
     all_sent(ids.at[chip, k], is_sem)
     all_sent(ids.at[pl.ds(0, 63)], i_s)
     all_sent(wbuf.at[pl.ds(0, 15 * CHUNKS)], w_s)
@@ -421,14 +430,18 @@
 
 def per_device(token_ids, embedding, norm_gain, in_proj, short_taps, conv_taps, out_proj):
     vmem = pl.BlockSpec(memory_space=pltpu.VMEM)
-    hbm = pl.BlockSpec(memory_space=pl.ANY)
+    hbm = pl.BlockSpec(memory_space=pltpu.HBM)
     dma = pltpu.SemaphoreType.DMA
     out = pl.pallas_call(
         kernel,
         out_shape=jax.ShapeDtypeStruct((128, D), BF16),
-        in_specs=[vmem, vmem, vmem, vmem, hbm, hbm, hbm],
-        out_specs=hbm,
+        in_specs=[hbm] * 7,
+        out_specs=vmem,
         scratch_shapes=[
+            pltpu.VMEM((1, 128), jnp.int32),
+            pltpu.VMEM((1, D), F32),
+            pltpu.VMEM((SHORT, 3, 128), F32),
+            pltpu.VMEM((8, 128), BF16),
             pltpu.VMEM((VOCAB, D), BF16),
             pltpu.VMEM((3, D, 128), BF16),
             pltpu.VMEM((VOCAB, D), BF16),
@@ -451,15 +464,18 @@
             pltpu.VMEM((CHUNKS, 2, 2, 128, CW), BF16),
             pltpu.VMEM((2, CHUNKS, 2, 128, CW), BF16),
             pltpu.VMEM((128, D), BF16),
-            pltpu.VMEM((128, D), BF16),
-            dma((3,)), dma((N_ONE,)), dma((CHUNKS, 5)), dma((2, 4)), dma((2, 4)),
+            dma((7,)), dma((N_ONE,)), dma((CHUNKS, 5)), dma((2, 4)), dma((2, 4)),
             dma((CHUNKS, 2)), dma((CHUNKS,)), dma((CHUNKS,)),
         ],
         compiler_params=pltpu.CompilerParams(
-            collective_id=0, has_side_effects=True, vmem_limit_bytes=60 * 1024 * 1024
+            collective_id=0, has_side_effects=True, vmem_limit_bytes=46 * 1024 * 1024
         ),
         name="mixer",
-    )(token_ids, norm_gain.reshape(1, D), short_taps, conv_taps, embedding, in_proj, out_proj)
+    )(*(
+        pltpu.with_memory_space_constraint(v, pltpu.HBM)
+        for v in (token_ids, norm_gain.reshape(1, D), short_taps, conv_taps, embedding,
+                  in_proj, out_proj)
+    ))
     return out[None]
 
 

time: 77.5 us -> 74 us (0.955)
  Pallas kernels: 75 us -> 73 us
  local copies, waits for them, and re-layouts: 2.29 us -> 0.97 us
    pallas_call x1, Pallas kernels: 75 us -> 73 us  [per_device(): pl.pallas_call(kernel, out_shape=jax.ShapeDtypeStruct((128, D), BF16), in...]
    unnamed x1, local copies, waits for them, and re-layouts: 2.29 us -> 0.97 us
where the time goes in v3:
time: 74 us; the launch traced here: 73.9 us
  Pallas kernels  73 us (99%)
  local copies, waits for them, and re-layouts  0.97 us (1%)
    pallas_call x1, Pallas kernels, per_device(): pl.pallas_call(kernel, out_shape=jax.ShapeDtypeStruct((128, D), BF16), in...  73 us

profile of v3, /device:TPU:1, one launch (start us, length us, event | category | flops | bytes accessed | tf_op | source)
XLA Modules:
  0.0 73.9 jit_solution(12516678199265550625)
XLA Ops:
  0.0 73.0 %mixer.1 = bf16[128,4096]{1,0:T(8,128)(2,1)S(1)} custom-call(s32[1,128]{1,0:T(1,128)} %ids_in.1, f32[1,4096]{1,0:T(1,128)} %bitcast.3, f32[3,3,128]{2,1,0:T(4,128)} %staps_in.1, bf16[8,128]{1,0:T(8,128)(2,1)} %ctaps_in.1, bf16[512,4096]{1,0:T(8,128)(2,1)} %emb_ref.1, bf16[3,4096,128]{2,1,0:T(8,128)(2,1)} %inp_ref.1, bf16[128,4096]{1,0:T(8,128)(2,1)} %op_ref.1), custom_call_target="tpu_custom_call" | custom-call | tf_op jit(solution)/shard_map/mixer/pallas_call | solution.py:435
  73.0 1.0 %copy.9 = bf16[1,128,4096]{2,1,0:T(8,128)(2,1)} copy(bf16[1,128,4096]{2,1,0:T(8,128)(2,1)S(1)} %bitcast.2) | data formatting | bytes 2097152

commit v4 on v3

--- a/solution.py
+++ b/solution.py
@@ -170,6 +170,10 @@
         src, dst = w_source(j), piece(j, p, q)
         w_send(j, PA, src, dst, 1, 0)
         w_send(j, PB, src, dst, 3, 0)
+
+    def stage1q(j):
+        p, q = coords(j)
+        src, dst = w_source(j), piece(j, p, q)
         w_send(j, QA, src, dst, 0, 1)
         w_send(j, QB, src, dst, 0, 3)
 
@@ -225,12 +229,14 @@
     arrived(ids.at[chip, 1 - k], ir_sem)
     for d in chips:
         send(ids.at[chip], ids.at[chip], i_s, i_r, chip_dev(*d))
+    stage1q(0)
+    stage1q(1)
     lax.fori_loop(4, 16, norm_rows, 0)
+    stage2(0)
+    stage2(1)
     table = dot_t(sel[...], normed[...]).astype(BF16)
     tab[0 : 3 * CH, :] = table[:, 0:256]
     tab[3 * CH : 6 * CH, :] = table[:, 256:512]
-    stage2(0)
-    stage2(1)
 
     own_hot = lax.broadcasted_iota(jnp.int32, (VOCAB, 128), 0) == ids_ref[...]
     own_hot = jnp.where(own_hot, 1.0, 0.0).astype(F32).T.astype(BF16)
@@ -302,7 +308,7 @@
                  gath.at[line, my_rows, half_lanes[t]],
                  g_s, g_r.at[t, dy], plane_dev(dy, dz))
 
-    polls = {2: lambda: (None,),1: lambda: (stage3(0),stage3(1),),3: lambda: (stage4(0),stage4(1),),0: lambda: (stage5(0),stage5(1),)}
+    polls = {2: lambda: (stage3(0),stage3(1),),1: lambda: (stage4(0),stage4(1),),3: lambda: (None,),0: lambda: (stage5(0),stage5(1),)}
     for dy in (2, 1, 3, 0):
         mix_rows(add(y, dy))
         scatter(dy, 0)
@@ -391,6 +397,8 @@
     w_ready(1)
     multiply(0, 1)
     pass_on(0, 0)
+    stage1q(2)
+    stage1q(3)
     pass_on(0, 1)
     hand_over(1)
     stage2(2)

time: 74 us -> 73.2 us (0.989)
  Pallas kernels: 73 us -> 72.1 us
    pallas_call x1, Pallas kernels: 73 us -> 72.1 us  [per_device(): pl.pallas_call(kernel, out_shape=jax.ShapeDtypeStruct((128, D), BF16), in...]
where the time goes in v4:
time: 73.2 us; the launch traced here: 73.1 us
  Pallas kernels  72.1 us (98%)
  local copies, waits for them, and re-layouts  0.97 us (1%)
    pallas_call x1, Pallas kernels, per_device(): pl.pallas_call(kernel, out_shape=jax.ShapeDtypeStruct((128, D), BF16), in...  72.1 us

profile of v4, /device:TPU:1, one launch (start us, length us, event | category | flops | bytes accessed | tf_op | source)
XLA Modules:
  0.0 73.1 jit_solution(3594788148315106164)
XLA Ops:
  0.0 72.1 %mixer.1 = bf16[128,4096]{1,0:T(8,128)(2,1)S(1)} custom-call(s32[1,128]{1,0:T(1,128)} %ids_in.1, f32[1,4096]{1,0:T(1,128)} %bitcast.3, f32[3,3,128]{2,1,0:T(4,128)} %staps_in.1, bf16[8,128]{1,0:T(8,128)(2,1)} %ctaps_in.1, bf16[512,4096]{1,0:T(8,128)(2,1)} %emb_ref.1, bf16[3,4096,128]{2,1,0:T(8,128)(2,1)} %inp_ref.1, bf16[128,4096]{1,0:T(8,128)(2,1)} %op_ref.1), custom_call_target="tpu_custom_call" | custom-call | tf_op jit(solution)/shard_map/mixer/pallas_call | solution.py:443
  72.1 1.0 %copy.9 = bf16[1,128,4096]{2,1,0:T(8,128)(2,1)} copy(bf16[1,128,4096]{2,1,0:T(8,128)(2,1)S(1)} %bitcast.2) | data formatting | bytes 2097152

commit v5 on v4

--- a/solution.py
+++ b/solution.py
@@ -423,9 +423,11 @@
     multiply(1, 3)
     pass_on(1, 2)
     pass_on(0, 3)
+    finish(0)
+    finish(1)
     pass_on(1, 3)
-    for j in range(CHUNKS):
-        finish(j)
+    finish(2)
+    finish(3)
     all_sent(ids.at[chip, k], is_sem)
     all_sent(ids.at[pl.ds(0, 63)], i_s)
     all_sent(wbuf.at[pl.ds(0, 15 * CHUNKS)], w_s)

time: 73.2 us -> 73.2 us (level)
  no operation moved by 1% of the time
where the time goes in v5:
time: 73.2 us; the launch traced here: 73.1 us
  Pallas kernels  72.1 us (98%)
  local copies, waits for them, and re-layouts  0.97 us (1%)
    pallas_call x1, Pallas kernels, per_device(): pl.pallas_call(kernel, out_shape=jax.ShapeDtypeStruct((128, D), BF16), in...  72.1 us

profile of v5, /device:TPU:1, one launch (start us, length us, event | category | flops | bytes accessed | tf_op | source)
XLA Modules:
  0.0 73.1 jit_solution(7260086742150464109)
XLA Ops:
  0.0 72.1 %mixer.1 = bf16[128,4096]{1,0:T(8,128)(2,1)S(1)} custom-call(s32[1,128]{1,0:T(1,128)} %ids_in.1, f32[1,4096]{1,0:T(1,128)} %bitcast.3, f32[3,3,128]{2,1,0:T(4,128)} %staps_in.1, bf16[8,128]{1,0:T(8,128)(2,1)} %ctaps_in.1, bf16[512,4096]{1,0:T(8,128)(2,1)} %emb_ref.1, bf16[3,4096,128]{2,1,0:T(8,128)(2,1)} %inp_ref.1, bf16[128,4096]{1,0:T(8,128)(2,1)} %op_ref.1), custom_call_target="tpu_custom_call" | custom-call | tf_op jit(solution)/shard_map/mixer/pallas_call | solution.py:445
  72.1 1.0 %copy.9 = bf16[1,128,4096]{2,1,0:T(8,128)(2,1)} copy(bf16[1,128,4096]{2,1,0:T(8,128)(2,1)S(1)} %bitcast.2) | data formatting | bytes 2097152
